TPU v7x, 512 devices: a whole 4x8x8 slice. The times are simulated.
512 devices in a mesh: row: 16 (over z, core), col: 32 (over x, y).
Axes of the slice: x: 4, y: 8, z: 8, core: 2. Of those that a mesh axis runs over, the one named last changes fastest.
Arguments:
- panel: bfloat16 [64, 1024, 256], P('row', 'col'), may hold values from -6 to 6
- inverse_factor: bfloat16 [1024, 1024], P('row', 'col'), as said below
- ranks: int32 [64], replicated, may hold values from 32 to 256
Outputs:
- solved: bfloat16 [64, 1024, 256], P('row', 'col')
- core_blocks: bfloat16 [64, 64, 256, 256], P('row', 'col')
Inputs may be any that keep to these rules, and one draw needn't show every extreme that they name: inverse_factor is lower triangular with a diagonal between 0.5 and 3.
All inputs are finite; a program needn't handle non-finite values.
Results may differ from a plain program's by a relative error of at most 0.017.
Values may be sent and summed in bfloat16 or wider, within the bound.
No kernel may reach another device: no remote copies, remote signals or barrier semaphores. Data moves between devices by JAX's collectives and lax.ppermute only.
A program may use at most 64 MiB of HBM per device.

v0:
```python
import jax
import jax.numpy as jnp
from jax import lax
from jax.sharding import Mesh
from jax.sharding import PartitionSpec as P

ROW = ("z", "core")
COL = ("x", "y")
ALL = ROW + COL


def size_of(axes):
    axes = axes if isinstance(axes, tuple) else (axes,)
    count = 1
    for axis in axes:
        count *= lax.axis_size(axis)
    return count


def sent_to_all(value, axes):
    copies = jnp.broadcast_to(value, (size_of(axes), *value.shape))
    return lax.all_to_all(copies, axes, split_axis=0, concat_axis=0, tiled=True)


def kept(value, ranks):
    columns = jnp.arange(value.shape[-1], dtype=jnp.int32)
    return value * (columns[None, :] < ranks[:, None]).astype(value.dtype)[:, None, :]


def column_tiles(panel, col, rows, cols):
    odd = lax.rem(col, 2)
    pair = panel.shape[0] // 2

    def moved(flip):
        half = lax.bitwise_xor(odd, flip)
        part = lax.dynamic_slice_in_dim(panel, pair * half, pair, 0)
        pairs = [
            (r * cols + c, c // 2 * cols + 2 * r + (c % 2 ^ flip))
            for r in range(rows)
            for c in range(cols)
        ]
        return lax.ppermute(part, ALL, pairs)

    first, second = (moved(0), moved(1))
    low = jnp.where(odd == 0, first, second)
    high = jnp.where(odd == 0, second, first)
    return jnp.concatenate([low, high], axis=1)


def per_device(panel, inverse_factor, ranks):
    tiles, depth, width = panel.shape
    core = lax.axis_index("core")
    row = lax.axis_index(ROW)
    col = lax.axis_index(COL)
    rows, cols = (size_of(ROW), size_of(COL))
    pair = tiles * rows // cols
    part = column_tiles(panel, col, rows, cols)
    factor = lax.all_gather(inverse_factor.T, "core", axis=1, tiled=True)
    half = depth // 2
    lanes = factor.shape[1]
    factor = lax.dynamic_slice_in_dim(factor, half * core, half, 0)
    factor = sent_to_all(factor, COL)
    part_rows = part.shape[1]
    sides = width // lanes
    packed = jnp.concatenate(
        [
            factor.reshape(cols * half, lanes),
            jnp.moveaxis(part.reshape(pair, part_rows, sides, lanes), 2, 0).reshape(-1, lanes),
        ],
        axis=0,
    )
    packed = lax.all_gather(packed, ROW)
    count = cols * half
    whole = packed[:, :count].reshape(rows // 2, 2, cols, half, lanes)
    whole = whole.transpose(2, 1, 3, 0, 4).reshape(cols * depth, -1)
    mine = packed[:, count:].reshape(rows, sides, pair, part_rows, lanes)
    mine = mine.transpose(2, 0, 3, 1, 4).reshape(pair, rows * part_rows, width)
    full = sent_to_all(sent_to_all(panel, "y"), "x")
    full = full.reshape(cols, tiles, depth, width).transpose(1, 0, 2, 3)
    full = full.reshape(tiles, cols * depth, width)
    full = kept(full, lax.dynamic_slice_in_dim(ranks, row * tiles, tiles, 0))
    mine = kept(mine, lax.dynamic_slice_in_dim(ranks, col * pair, pair, 0))

    def solve(value):
        out = jnp.einsum("ba,tbr->tar", whole, value, preferred_element_type=jnp.float32)
        return out.astype(jnp.bfloat16)

    solved_full = solve(full)
    solved_mine = solve(mine)
    shares = lax.dynamic_slice_in_dim(solved_full, col * depth, depth, 1)
    core_blocks = jnp.einsum(
        "tar,uas->turs", solved_full, solved_mine, preferred_element_type=jnp.float32
    ).astype(jnp.bfloat16)
    return (shares, core_blocks)


def solution(mesh):
    split = Mesh(mesh.devices.reshape(8, 2, 4, 8), ALL)
    return jax.shard_map(
        per_device,
        mesh=split,
        in_specs=(P(ROW, COL, None), P(ROW, COL), P()),
        out_specs=(P(ROW, COL, None), P(ROW, COL, None, None)),
        check_vma=False,
    )
```

profile of v0, /device:TPU:128, one launch (start us, length us, event | category | flops | bytes accessed | tf_op | source)
XLA Modules:
  0.0 129.7 jit_solution(5983271142760320367)
XLA Ops:
  7.2 0.8 constant_dynamic-slice_fusion.1
  8.0 1.9 %collective-permute-start = (bf16[2,32,256]{2,1,0:T(8,128)(2,1)S(1)}, bf16[2,32,256]{2,1,0:T(8,128)(2,1)S(1)}, u32[]{:S(2)}, u32[]{:S(2)}) collective-permute-start(bf16[2,32,256]{2,1,0:T(8,128)(2,1)S(1)} %get-tuple-element.12), channel_id=1, source_target_pairs={{0,0},{1,1},{2,32},{3,33},{4,64},{5,65},{6,96},{7,97},{8,128},{9,1... | collective-permute-start | bytes 98312 | tf_op jit(solution)/shard_map/ppermute | solution.py:42
  9.9 6.7 %collective-permute-start.1 = (bf16[2,32,256]{2,1,0:T(8,128)(2,1)S(1)}, bf16[2,32,256]{2,1,0:T(8,128)(2,1)S(1)}, u32[]{:S(2)}, u32[]{:S(2)}) collective-permute-start(bf16[2,32,256]{2,1,0:T(8,128)(2,1)S(1)} %get-tuple-element.13), channel_id=1, source_target_pairs={{0,1},{1,0},{2,33},{3,32},{4,65},{5,64},{6,97},{7,96},{8,129},{9,1... | collective-permute-start | bytes 98312 | tf_op jit(solution)/shard_map/ppermute | solution.py:42
  16.6 3.0 %all-gather.1 = bf16[2,64,32]{1,2,0:T(8,128)(2,1)S(1)} all-gather(bf16[1,64,32]{1,2,0:T(8,128)(2,1)} %bitcast.55), channel_id=1, replica_groups=mesh['z'=8,'core'=2,'x'=4,'y'=8] {'core'}, dimensions={0}, use_global_device_ids=true | all-gather | bytes 12288 | tf_op jit(solution)/shard_map/all_gather | solution.py:58
  19.7 0.1 reshape.76
  19.8 0.7 broadcast_in_dim.8
  20.5 15.3 %all-to-all-start.2 = ((bf16[32,16,128]{2,1,0:T(8,128)(2,1)}), bf16[32,16,128]{2,1,0:T(8,128)(2,1)S(1)}, u32[]{:S(2)}, u32[]{:S(2)}) async-start(bf16[32,16,128]{2,1,0:T(8,128)(2,1)} %broadcast_in_dim.8), calls=%async_computation.2 | async-start | bytes 262144 | tf_op jit(solution)/shard_map/all_to_all | solution.py:22
  35.8 0.0 all-gather.4.cloned.1.call-start
  35.8 0.0 collective-permute-done
  35.8 0.0 collective-permute-done.1
  35.9 10.5 %all-to-all-done.2 = bf16[32,16,128]{2,1,0:T(8,128)(2,1)S(1)} async-done(((bf16[32,16,128]{2,1,0:T(8,128)(2,1)}), bf16[32,16,128]{2,1,0:T(8,128)(2,1)S(1)}, u32[]{:S(2)}, u32[]{:S(2)}) %all-to-all-start.2) | async-done | bytes 131104 | tf_op jit(solution)/shard_map/all_to_all | solution.py:22
  46.4 0.7 pad_maximum_fusion
  47.1 0.0 all-gather.4.cloned.1.call-update
  47.1 0.9 broadcast_in_dim.6
  48.0 19.4 %all_to_all.15 = bf16[8,4,32,256]{3,2,1,0:T(8,128)(2,1)S(1)} all-to-all(bf16[8,4,32,256]{3,2,1,0:T(8,128)(2,1)S(1)} %broadcast_in_dim.6), channel_id=1, replica_groups=mesh['z'=8,'core'=2,'x'=4,'y'=8] {'y'}, dimensions={0} | all-to-all | bytes 1048576 | tf_op jit(solution)/shard_map/all_to_all | solution.py:22
  67.4 1.6 %broadcast_in_dim.7 = bf16[4,8,4,32,256]{4,3,1,2,0:T(8,128)(2,1)} broadcast(bf16[8,4,32,256]{3,2,0,1:T(8,128)(2,1)S(1)} %copy.26), dimensions={1,2,3,4} | broadcast | bytes 2621440 | tf_op jit(solution)/shard_map/broadcast_in_dim | solution.py:21
  69.1 0.0 copy-start.1
  69.1 3.7 %all-to-all-start.1 = ((bf16[4,8,4,32,256]{4,3,1,2,0:T(8,128)(2,1)}), bf16[4,8,4,32,256]{4,3,1,2,0:T(8,128)(2,1)S(1)}, u32[]{:S(2)}, u32[]{:S(2)}) async-start(bf16[4,8,4,32,256]{4,3,1,2,0:T(8,128)(2,1)} %broadcast_in_dim.7), calls=%async_computation.1 | async-start | bytes 4194304 | tf_op jit(solution)/shard_map/all_to_all | solution.py:22
  72.8 0.0 copy-done.1
  72.9 0.1 dynamic_slice.23
  72.9 0.1 dynamic_slice.18
  73.0 0.1 fusion.9
  73.1 0.1 compare_convert_fusion
  73.2 23.9 %all-to-all-done.1 = bf16[4,8,4,32,256]{4,3,1,2,0:T(8,128)(2,1)S(1)} async-done(((bf16[4,8,4,32,256]{4,3,1,2,0:T(8,128)(2,1)}), bf16[4,8,4,32,256]{4,3,1,2,0:T(8,128)(2,1)S(1)}, u32[]{:S(2)}, u32[]{:S(2)}) %all-to-all-start.1) | async-done | bytes 2097184 | tf_op jit(solution)/shard_map/all_to_all | solution.py:22
  97.1 0.2 copy.27
  97.3 1.5 %broadcast_multiply_fusion = bf16[32,4,32,256]{3,2,0,1:T(8,128)(2,1)} fusion(bf16[32,4,32,256]{3,2,0,1:T(8,128)(2,1)S(1)} %bitcast.46, bf16[4,256]{1,0:T(4,128)(2,1)S(1)} %fusion.9), kind=kLoop, calls=%fused_computation.8 | loop fusion | flops 1048576 | bytes 4196352 | tf_op jit(solution)/shard_map/mul | solution.py:27
  98.8 0.0 all-gather.4.cloned.1.call-done
  98.8 1.3 slice.9
  100.1 1.8 %slice.8 = bf16[16,512,128]{2,1,0:T(8,128)(2,1)S(1)} slice(bf16[16,768,128]{2,1,0:T(8,128)(2,1)} %bitcast.50), slice={[0:16], [0:512], [0:128]} | slice | bytes 4194304 | tf_op jit(solution)/shard_map/slice | solution.py:74
  101.8 2.4 %copy.30 = bf16[32,2,16,8,128]{4,3,2,1,0:T(8,128)(2,1)S(1)} copy(bf16[32,2,16,8,128]{4,2,0,1,3:T(8,128)(2,1)S(1)} %bitcast.47) | data formatting | bytes 4194304 | tf_op jit(solution)/shard_map/transpose | solution.py:75
  104.3 2.3 %reshape.77 = bf16[1024,1024,1]{1,0,2:T(8,128)(2,1)} reshape(bf16[32,2,16,8,128]{4,3,2,1,0:T(8,128)(2,1)S(1)} %copy.30) | data formatting | bytes 4194304 | tf_op jit(solution)/shard_map/reshape | solution.py:75
  106.6 1.2 bitcast_multiply_fusion
  107.8 1.5 %mul.59 = bf16[2,1024,256]{2,1,0:T(8,128)(2,1)} reshape(bf16[2,16,64,2,128]{4,3,2,1,0:T(2,128)(2,1)S(1)} %bitcast_multiply_fusion) | data formatting | bytes 2097152 | tf_op jit(solution)/shard_map/mul | solution.py:27
  109.3 0.0 copy-start
  109.3 6.1 %convolution_convert_fusion = bf16[4,256,1024]{2,1,0:T(8,128)(2,1)} fusion(bf16[4,1024,256]{2,1,0:T(8,128)(2,1)} %bitcast.51, bf16[1024,1024,1]{1,0,2:T(8,128)(2,1)} %reshape.77), kind=kOutput, calls=%fused_computation.2 | convolution fusion | flops 2148532224 | bytes 6291456 | tf_op jit(solution)/shard_map/ba,tbr->tar/dot_general | solution.py:85
  115.4 0.0 copy-done
  115.4 4.3 %fusion.6 = bf16[4,2,256,256]{2,3,0,1:T(8,128)(2,1)S(1)} fusion(bf16[4,256,1024]{2,1,0:T(8,128)(2,1)} %convolution_convert_fusion, bf16[2,1024,256]{2,1,0:T(8,128)(2,1)} %mul.59, bf16[1024,1024,1]{1,0,2:T(8,128)(2,1)S(1)} %copy-done), kind=kOutput, calls=%fused_computation.6 | convolution fusion | flops 2148532224 | bytes 6291456 | tf_op jit(solution)/shard_map/tar,uas->turs/dot_general | solution.py:91
  119.7 1.1 dynamic-slice_bitcast_fusion
  120.8 0.8 copy.35
  121.6 1.3 %copy.36 = bf16[4,2,256,256]{3,2,1,0:T(8,128)(2,1)} copy(bf16[4,2,256,256]{2,3,0,1:T(8,128)(2,1)S(1)} %fusion.6) | data formatting | bytes 2097152
  (8 shorter events, 0.1 us)
Async XLA Ops:
  8.0 27.9 %collective-permute-start = (bf16[2,32,256]{2,1,0:T(8,128)(2,1)S(1)}, bf16[2,32,256]{2,1,0:T(8,128)(2,1)S(1)}, u32[]{:S(2)}, u32[]{:S(2)}) collective-permute-start(bf16[2,32,256]{2,1,0:T(8,128)(2,1)S(1)} %get-tuple-element.12), channel_id=1, source_target_pairs={{0,0},{1,1},{2,32},{3,33},{4,64},{5,65},{6,96},{7,97},{8,128},{9,1... | collective-permute-start | bytes 98312 | tf_op jit(solution)/shard_map/ppermute | solution.py:42
  9.9 25.9 %collective-permute-start.1 = (bf16[2,32,256]{2,1,0:T(8,128)(2,1)S(1)}, bf16[2,32,256]{2,1,0:T(8,128)(2,1)S(1)}, u32[]{:S(2)}, u32[]{:S(2)}) collective-permute-start(bf16[2,32,256]{2,1,0:T(8,128)(2,1)S(1)} %get-tuple-element.13), channel_id=1, source_target_pairs={{0,1},{1,0},{2,33},{3,32},{4,65},{5,64},{6,97},{7,96},{8,129},{9,1... | collective-permute-start | bytes 98312 | tf_op jit(solution)/shard_map/ppermute | solution.py:42
  20.5 25.9 %all-to-all-start.2 = ((bf16[32,16,128]{2,1,0:T(8,128)(2,1)}), bf16[32,16,128]{2,1,0:T(8,128)(2,1)S(1)}, u32[]{:S(2)}, u32[]{:S(2)}) async-start(bf16[32,16,128]{2,1,0:T(8,128)(2,1)} %broadcast_in_dim.8), calls=%async_computation.2 | async-start | bytes 262144 | tf_op jit(solution)/shard_map/all_to_all | solution.py:22
  35.8 63.0 %all-gather.4.cloned.1.call-start = ((), (), s32[]{:S(2)}) async-start(), calls=%async_computation.3 | async-start | bytes 3342336 | tf_op jit(solution)/shard_map/all_gather | solution.py:72
  69.1 3.8 %copy-start.1 = (s32[64]{0:T(128)S(1)}, s32[64]{0:T(128)}, u32[]{:S(2)}) copy-start(s32[64]{0:T(128)} %param.5) | copy-start | bytes 772
  69.1 28.0 %all-to-all-start.1 = ((bf16[4,8,4,32,256]{4,3,1,2,0:T(8,128)(2,1)}), bf16[4,8,4,32,256]{4,3,1,2,0:T(8,128)(2,1)S(1)}, u32[]{:S(2)}, u32[]{:S(2)}) async-start(bf16[4,8,4,32,256]{4,3,1,2,0:T(8,128)(2,1)} %broadcast_in_dim.7), calls=%async_computation.1 | async-start | bytes 4194304 | tf_op jit(solution)/shard_map/all_to_all | solution.py:22
  109.3 6.1 %copy-start = (bf16[1024,1024,1]{1,0,2:T(8,128)(2,1)S(1)}, bf16[1024,1024,1]{1,0,2:T(8,128)(2,1)}, u32[]{:S(2)}) copy-start(bf16[1024,1024,1]{1,0,2:T(8,128)(2,1)} %reshape.77) | copy-start | bytes 6291460
Sparse Core Ops, SparseCore 0:
  47.2 37.9 all-gather.3
where the time goes:
time: 130 us
  waiting for transfers between devices  34.4 us (26%)
  starting transfers between devices  27.7 us (21%)
  blocking collectives  22.4 us (17%)
  local copies, waits for them, and re-layouts  16.9 us (13%)
  between operations  14.2 us (11%)
  matrix products  10.4 us (8%)
  other arithmetic  3.59 us (3%)
    all_to_all x2, waiting for transfers between devices, sent_to_all(): return lax.all_to_all(copies, axes, split_axis=0, concat_axis=0, tiled=True)  34.4 us
    all_to_all x1, blocking collectives, sent_to_all(): return lax.all_to_all(copies, axes, split_axis=0, concat_axis=0, tiled=True)  19.4 us
    all_to_all x2, starting transfers between devices, sent_to_all(): return lax.all_to_all(copies, axes, split_axis=0, concat_axis=0, tiled=True)  19 us
    ppermute x2, starting transfers between devices, moved(): return lax.ppermute(part, ALL, pairs)  8.64 us
    dot_general x1, matrix products, solve(): jnp.einsum('ba,tbr->tar', whole, value, preferred_element_type=jnp.float32)  6.11 us
    dot_general x1, matrix products, per_device(): jnp.einsum('tar,uas->turs', solved_full, solved_mine, preferred_element_t...  4.27 us
    broadcast_in_dim x3, local copies, waits for them, and re-layouts, sent_to_all(): copies = jnp.broadcast_to(value, (size_of(axes), *value.shape))  3.21 us
    all_gather x1, blocking collectives, per_device(): factor = lax.all_gather(inverse_factor.T, 'core', axis=1, tiled=True)  3.04 us
  transfers between devices with their start and end apart: 5, of which 2 were waited for; matrix products, arithmetic and copies ran while one was open for 4% of the time, Pallas kernels for 0%

commit v1 on v0

--- a/solution.py
+++ b/solution.py
@@ -7,6 +7,11 @@
 ROW = ("z", "core")
 COL = ("x", "y")
 ALL = ROW + COL
+
+
+def gather_over(array, name, along):
+    sent = jnp.stack([array] * lax.axis_size(name))
+    return jnp.concatenate(lax.all_to_all(sent, name, 0, 0), axis=along)
 
 
 def size_of(axes):
@@ -55,7 +60,7 @@
     rows, cols = (size_of(ROW), size_of(COL))
     pair = tiles * rows // cols
     part = column_tiles(panel, col, rows, cols)
-    factor = lax.all_gather(inverse_factor.T, "core", axis=1, tiled=True)
+    factor = gather_over(inverse_factor.T, "core", 1)
     half = depth // 2
     lanes = factor.shape[1]
     factor = lax.dynamic_slice_in_dim(factor, half * core, half, 0)

time: 130 us -> 135 us (1.038)
  the two profiles are of different devices: /device:TPU:128 before, /device:TPU:64 now
where the time goes in v1:
time: 135 us; the launch traced here: 134 us
  waiting for transfers between devices  36.6 us (27%)
  starting transfers between devices  29.2 us (22%)
  blocking collectives  21.7 us (16%)
  local copies, waits for them, and re-layouts  17.7 us (13%)
  between operations  14.2 us (11%)
  matrix products  10.4 us (8%)
  other arithmetic  4.38 us (3%)
    all_to_all x2, waiting for transfers between devices, sent_to_all(): return lax.all_to_all(copies, axes, split_axis=0, concat_axis=0, tiled=True)  36.6 us
    all_to_all x1, blocking collectives, sent_to_all(): return lax.all_to_all(copies, axes, split_axis=0, concat_axis=0, tiled=True)  21.7 us
    all_to_all x2, starting transfers between devices, sent_to_all(): return lax.all_to_all(copies, axes, split_axis=0, concat_axis=0, tiled=True)  15.2 us
    ppermute x2, starting transfers between devices, moved(): return lax.ppermute(part, ALL, pairs)  10.8 us
    dot_general x1, matrix products, solve(): jnp.einsum('ba,tbr->tar', whole, value, preferred_element_type=jnp.float32)  6.12 us
    dot_general x1, matrix products, per_device(): jnp.einsum('tar,uas->turs', solved_full, solved_mine, preferred_element_t...  4.27 us
    all_to_all x1, starting transfers between devices, gather_over(): return jnp.concatenate(lax.all_to_all(sent, name, 0, 0), axis=along)  3.23 us
    broadcast_in_dim x3, local copies, waits for them, and re-layouts, sent_to_all(): copies = jnp.broadcast_to(value, (size_of(axes), *value.shape))  3.21 us
  transfers between devices with their start and end apart: 6, of which 2 were waited for; matrix products, arithmetic and copies ran while one was open for 5% of the time, Pallas kernels for 0%

profile of v1, /device:TPU:64, one launch (start us, length us, event | category | flops | bytes accessed | tf_op | source)
XLA Modules:
  0.0 134.2 jit_solution(3589659635594121485)
XLA Ops:
  7.2 0.8 pad_maximum_fusion.2
  7.9 0.7 reshape.87
  8.6 3.2 %all-to-all-start.2 = ((bf16[2,2,1024]{2,1,0:T(2,128)(2,1)}), bf16[2,2,1024]{2,1,0:T(2,128)(2,1)S(1)}, u32[]{:S(2)}, u32[]{:S(2)}) async-start(bf16[2,2,1024]{2,1,0:T(2,128)(2,1)} %reshape.87), calls=%async_computation.2 | async-start | bytes 16384 | tf_op jit(solution)/shard_map/all_to_all | solution.py:14
  11.9 0.8 constant_dynamic-slice_fusion.1
  12.7 6.8 %collective-permute-start = (bf16[2,32,256]{2,1,0:T(8,128)(2,1)S(1)}, bf16[2,32,256]{2,1,0:T(8,128)(2,1)S(1)}, u32[]{:S(2)}, u32[]{:S(2)}) collective-permute-start(bf16[2,32,256]{2,1,0:T(8,128)(2,1)S(1)} %get-tuple-element.12), channel_id=1, source_target_pairs={{0,0},{1,1},{2,32},{3,33},{4,64},{5,65},{6,96},{7,97},{8,128},{9,1... | collective-permute-start | bytes 98312 | tf_op jit(solution)/shard_map/ppermute | solution.py:47
  19.5 3.9 %collective-permute-start.1 = (bf16[2,32,256]{2,1,0:T(8,128)(2,1)S(1)}, bf16[2,32,256]{2,1,0:T(8,128)(2,1)S(1)}, u32[]{:S(2)}, u32[]{:S(2)}) collective-permute-start(bf16[2,32,256]{2,1,0:T(8,128)(2,1)S(1)} %get-tuple-element.13), channel_id=1, source_target_pairs={{0,1},{1,0},{2,33},{3,32},{4,65},{5,64},{6,97},{7,96},{8,129},{9,1... | collective-permute-start | bytes 98312 | tf_op jit(solution)/shard_map/ppermute | solution.py:47
  23.4 0.0 all-to-all-done.2
  23.5 0.1 reshape.88
  23.6 0.1 reshape.75
  23.7 0.7 broadcast_in_dim.8
  24.3 11.5 %all-to-all-start.3 = ((bf16[32,16,128]{2,1,0:T(8,128)(2,1)}), bf16[32,16,128]{2,1,0:T(8,128)(2,1)S(1)}, u32[]{:S(2)}, u32[]{:S(2)}) async-start(bf16[32,16,128]{2,1,0:T(8,128)(2,1)} %broadcast_in_dim.8), calls=%async_computation.3 | async-start | bytes 262144 | tf_op jit(solution)/shard_map/all_to_all | solution.py:27
  35.8 0.0 all-gather.3.cloned.1.call-start
  35.8 0.0 collective-permute-done
  35.9 0.0 collective-permute-done.1
  35.9 10.2 %all-to-all-done.3 = bf16[32,16,128]{2,1,0:T(8,128)(2,1)S(1)} async-done(((bf16[32,16,128]{2,1,0:T(8,128)(2,1)}), bf16[32,16,128]{2,1,0:T(8,128)(2,1)S(1)}, u32[]{:S(2)}, u32[]{:S(2)}) %all-to-all-start.3) | async-done | bytes 131104 | tf_op jit(solution)/shard_map/all_to_all | solution.py:27
  46.1 0.7 pad_maximum_fusion
  46.8 0.0 all-gather.3.cloned.1.call-update
  46.8 0.9 broadcast_in_dim.6
  47.7 21.7 %all_to_all.20 = bf16[8,4,32,256]{3,2,1,0:T(8,128)(2,1)S(1)} all-to-all(bf16[8,4,32,256]{3,2,1,0:T(8,128)(2,1)S(1)} %broadcast_in_dim.6), channel_id=1, replica_groups=mesh['z'=8,'core'=2,'x'=4,'y'=8] {'y'}, dimensions={0} | all-to-all | bytes 1048576 | tf_op jit(solution)/shard_map/all_to_all | solution.py:27
  69.4 1.6 %broadcast_in_dim.7 = bf16[4,8,4,32,256]{4,3,1,2,0:T(8,128)(2,1)} broadcast(bf16[8,4,32,256]{3,2,0,1:T(8,128)(2,1)S(1)} %copy.25), dimensions={1,2,3,4} | broadcast | bytes 2621440 | tf_op jit(solution)/shard_map/broadcast_in_dim | solution.py:26
  71.1 0.0 copy-start.1
  71.1 3.7 %all-to-all-start.1 = ((bf16[4,8,4,32,256]{4,3,1,2,0:T(8,128)(2,1)}), bf16[4,8,4,32,256]{4,3,1,2,0:T(8,128)(2,1)S(1)}, u32[]{:S(2)}, u32[]{:S(2)}) async-start(bf16[4,8,4,32,256]{4,3,1,2,0:T(8,128)(2,1)} %broadcast_in_dim.7), calls=%async_computation.1 | async-start | bytes 4194304 | tf_op jit(solution)/shard_map/all_to_all | solution.py:27
  74.8 0.0 copy-done.1
  74.9 0.1 dynamic_slice.23
  74.9 0.1 dynamic_slice.18
  75.0 0.1 fusion.9
  75.1 0.1 compare_convert_fusion
  75.2 26.5 %all-to-all-done.1 = bf16[4,8,4,32,256]{4,3,1,2,0:T(8,128)(2,1)S(1)} async-done(((bf16[4,8,4,32,256]{4,3,1,2,0:T(8,128)(2,1)}), bf16[4,8,4,32,256]{4,3,1,2,0:T(8,128)(2,1)S(1)}, u32[]{:S(2)}, u32[]{:S(2)}) %all-to-all-start.1) | async-done | bytes 2097184 | tf_op jit(solution)/shard_map/all_to_all | solution.py:27
  101.6 0.2 copy.26
  101.8 1.5 %broadcast_multiply_fusion = bf16[32,4,32,256]{3,2,0,1:T(8,128)(2,1)} fusion(bf16[32,4,32,256]{3,2,0,1:T(8,128)(2,1)S(1)} %bitcast.45, bf16[4,256]{1,0:T(4,128)(2,1)S(1)} %fusion.9), kind=kLoop, calls=%fused_computation.8 | loop fusion | flops 1048576 | bytes 4196352 | tf_op jit(solution)/shard_map/mul | solution.py:32
  103.3 0.0 all-gather.3.cloned.1.call-done
  103.3 1.3 slice.9
  104.6 1.8 %slice.8 = bf16[16,512,128]{2,1,0:T(8,128)(2,1)S(1)} slice(bf16[16,768,128]{2,1,0:T(8,128)(2,1)} %bitcast.49), slice={[0:16], [0:512], [0:128]} | slice | bytes 4194304 | tf_op jit(solution)/shard_map/slice | solution.py:79
  106.4 2.4 %copy.29 = bf16[32,2,16,8,128]{4,3,2,1,0:T(8,128)(2,1)S(1)} copy(bf16[32,2,16,8,128]{4,2,0,1,3:T(8,128)(2,1)S(1)} %bitcast.46) | data formatting | bytes 4194304 | tf_op jit(solution)/shard_map/transpose | solution.py:80
  108.8 2.3 %reshape.83 = bf16[1024,1024,1]{1,0,2:T(8,128)(2,1)} reshape(bf16[32,2,16,8,128]{4,3,2,1,0:T(8,128)(2,1)S(1)} %copy.29) | data formatting | bytes 4194304 | tf_op jit(solution)/shard_map/reshape | solution.py:80
  111.1 1.2 bitcast_multiply_fusion
  112.4 1.5 %mul.59 = bf16[2,1024,256]{2,1,0:T(8,128)(2,1)} reshape(bf16[2,16,64,2,128]{4,3,2,1,0:T(2,128)(2,1)S(1)} %bitcast_multiply_fusion) | data formatting | bytes 2097152 | tf_op jit(solution)/shard_map/mul | solution.py:32
  113.8 0.0 copy-start
  113.8 6.1 %convolution_convert_fusion = bf16[4,256,1024]{2,1,0:T(8,128)(2,1)} fusion(bf16[4,1024,256]{2,1,0:T(8,128)(2,1)} %bitcast.50, bf16[1024,1024,1]{1,0,2:T(8,128)(2,1)} %reshape.83), kind=kOutput, calls=%fused_computation.2 | convolution fusion | flops 2148532224 | bytes 6291456 | tf_op jit(solution)/shard_map/ba,tbr->tar/dot_general | solution.py:90
  120.0 0.0 copy-done
  120.0 4.3 %fusion.6 = bf16[4,2,256,256]{2,3,0,1:T(8,128)(2,1)S(1)} fusion(bf16[4,256,1024]{2,1,0:T(8,128)(2,1)} %convolution_convert_fusion, bf16[2,1024,256]{2,1,0:T(8,128)(2,1)} %mul.59, bf16[1024,1024,1]{1,0,2:T(8,128)(2,1)S(1)} %copy-done), kind=kOutput, calls=%fused_computation.6 | convolution fusion | flops 2148532224 | bytes 6291456 | tf_op jit(solution)/shard_map/tar,uas->turs/dot_general | solution.py:96
  124.2 1.1 dynamic-slice_bitcast_fusion
  125.3 0.8 copy.34
  126.1 1.3 copy.35
  (8 shorter events, 0.1 us)
Async XLA Ops:
  8.6 14.8 %all-to-all-start.2 = ((bf16[2,2,1024]{2,1,0:T(2,128)(2,1)}), bf16[2,2,1024]{2,1,0:T(2,128)(2,1)S(1)}, u32[]{:S(2)}, u32[]{:S(2)}) async-start(bf16[2,2,1024]{2,1,0:T(2,128)(2,1)} %reshape.87), calls=%async_computation.2 | async-start | bytes 16384 | tf_op jit(solution)/shard_map/all_to_all | solution.py:14
  12.7 23.2 %collective-permute-start = (bf16[2,32,256]{2,1,0:T(8,128)(2,1)S(1)}, bf16[2,32,256]{2,1,0:T(8,128)(2,1)S(1)}, u32[]{:S(2)}, u32[]{:S(2)}) collective-permute-start(bf16[2,32,256]{2,1,0:T(8,128)(2,1)S(1)} %get-tuple-element.12), channel_id=1, source_target_pairs={{0,0},{1,1},{2,32},{3,33},{4,64},{5,65},{6,96},{7,97},{8,128},{9,1... | collective-permute-start | bytes 98312 | tf_op jit(solution)/shard_map/ppermute | solution.py:47
  19.5 16.4 %collective-permute-start.1 = (bf16[2,32,256]{2,1,0:T(8,128)(2,1)S(1)}, bf16[2,32,256]{2,1,0:T(8,128)(2,1)S(1)}, u32[]{:S(2)}, u32[]{:S(2)}) collective-permute-start(bf16[2,32,256]{2,1,0:T(8,128)(2,1)S(1)} %get-tuple-element.13), channel_id=1, source_target_pairs={{0,1},{1,0},{2,33},{3,32},{4,65},{5,64},{6,97},{7,96},{8,129},{9,1... | collective-permute-start | bytes 98312 | tf_op jit(solution)/shard_map/ppermute | solution.py:47
  24.3 21.8 %all-to-all-start.3 = ((bf16[32,16,128]{2,1,0:T(8,128)(2,1)}), bf16[32,16,128]{2,1,0:T(8,128)(2,1)S(1)}, u32[]{:S(2)}, u32[]{:S(2)}) async-start(bf16[32,16,128]{2,1,0:T(8,128)(2,1)} %broadcast_in_dim.8), calls=%async_computation.3 | async-start | bytes 262144 | tf_op jit(solution)/shard_map/all_to_all | solution.py:27
  35.8 67.5 %all-gather.3.cloned.1.call-start = ((), (), s32[]{:S(2)}) async-start(), calls=%async_computation.4 | async-start | bytes 3342336 | tf_op jit(solution)/shard_map/all_gather | solution.py:77
  71.1 3.8 %copy-start.1 = (s32[64]{0:T(128)S(1)}, s32[64]{0:T(128)}, u32[]{:S(2)}) copy-start(s32[64]{0:T(128)} %param.5) | copy-start | bytes 772
  71.1 30.5 %all-to-all-start.1 = ((bf16[4,8,4,32,256]{4,3,1,2,0:T(8,128)(2,1)}), bf16[4,8,4,32,256]{4,3,1,2,0:T(8,128)(2,1)S(1)}, u32[]{:S(2)}, u32[]{:S(2)}) async-start(bf16[4,8,4,32,256]{4,3,1,2,0:T(8,128)(2,1)} %broadcast_in_dim.7), calls=%async_computation.1 | async-start | bytes 4194304 | tf_op jit(solution)/shard_map/all_to_all | solution.py:27
  113.8 6.1 %copy-start = (bf16[1024,1024,1]{1,0,2:T(8,128)(2,1)S(1)}, bf16[1024,1024,1]{1,0,2:T(8,128)(2,1)}, u32[]{:S(2)}) copy-start(bf16[1024,1024,1]{1,0,2:T(8,128)(2,1)} %reshape.83) | copy-start | bytes 6291460
Sparse Core Ops, SparseCore 0:
  46.9 42.6 all-gather.2
